TPU v7x, 256 devices: a whole 4x4x8 slice. The times are simulated.
256 devices in a mesh: seq: 32 (over x, y, core), tensor: 8 (over z).
Axes of the slice: x: 4, y: 4, z: 8, core: 2. Of those that a mesh axis runs over, the one named last changes fastest.
Arguments:
- tokens: bfloat16 [16384, 4096], P('seq', 'tensor'), may hold values from -6 to 6
- norm_gain: float32 [4096], replicated, may hold values from 0.1 to 1.9
- w_query: bfloat16 [4096, 4096], P('seq', 'tensor'), may hold values from -0.09375 to 0.09375
- w_key: bfloat16 [4096, 4096], P('seq', 'tensor'), may hold values from -0.09375 to 0.09375
- w_value: bfloat16 [4096, 4096], P('seq', 'tensor'), may hold values from -0.09375 to 0.09375
- out_gain: float32 [4096], P('tensor'), may hold values from 0.1 to 1.9
- carried: float32 [32, 128, 128], P('tensor'), may hold values from -384 to 384
Outputs:
- attended: bfloat16 [16384, 4096], P('seq', 'tensor')
- final_state: float32 [32, 128, 128], P('tensor')
All inputs are finite; a program needn't handle non-finite values.
Results may differ from a plain program's by a relative error of at most 0.009.
Values may be sent and summed in bfloat16 or wider, within the bound.
No kernel may reach another device: no remote copies, remote signals or barrier semaphores. Data moves between devices by JAX's collectives and lax.ppermute only.
A program may use at most 64 MiB of HBM per device.

v0:
```python
import jax
import jax.numpy as jnp
from jax import lax
from jax.sharding import PartitionSpec as P

BLOCK = 512


def add_rows(normed, pieces):
    return tuple((jnp.dot(normed, piece, preferred_element_type=jnp.float32) for piece in pieces))


def shards(tokens, norm_gain, w_query, w_key, w_value, out_gain, carried):
    whole = lax.all_gather(tokens, "tensor", axis=1, tiled=True)
    xf = whole.astype(jnp.float32)
    normed = (xf * lax.rsqrt(jnp.mean(xf * xf, axis=1, keepdims=True) + 1e-05) * norm_gain).astype(
        jnp.bfloat16
    )
    rows = normed.shape[0]
    width = w_query.shape[1]
    size = carried.shape[1]
    heads = width // size
    qsum, ksum, vsum = add_rows(
        normed,
        (
            lax.all_gather(w_query, "seq", axis=0, tiled=True),
            lax.all_gather(w_key, "seq", axis=0, tiled=True),
            lax.all_gather(w_value, "seq", axis=0, tiled=True),
        ),
    )
    blocks = rows // BLOCK
    query = qsum.astype(jnp.bfloat16).reshape(blocks, BLOCK, heads, size)
    key = ksum.astype(jnp.bfloat16).reshape(blocks, BLOCK, heads, size)
    value = vsum.astype(jnp.bfloat16).reshape(blocks, BLOCK, heads, size)
    block_state = jnp.einsum("nthd,nthe->nhde", key, value, preferred_element_type=jnp.float32)
    local_total = jnp.sum(block_state, axis=0)
    zero_state = jnp.zeros_like(local_total)
    mine = lax.axis_index("seq")
    piece = lax.all_gather(
        local_total[None].astype(jnp.bfloat16), "seq", axis=0, tiled=True
    ).astype(jnp.float32)
    where = jnp.arange(piece.shape[0], dtype=jnp.int32)
    keep = (where < mine).astype(jnp.float32)
    before = zero_state + jnp.sum(keep[:, None, None, None] * piece, axis=0)
    total = zero_state + jnp.sum(piece, axis=0)
    start_state = carried + before
    running = jnp.cumsum(block_state, axis=0) - block_state
    priors = start_state[None] + running
    inter = jnp.einsum(
        "nthd,nhde->nthe", query.astype(jnp.float32), priors, precision=lax.Precision.HIGHEST
    )
    causal = jnp.tril(jnp.ones((BLOCK, BLOCK), jnp.float32))
    scores = jnp.einsum("nthd,nshd->nhts", query, key, preferred_element_type=jnp.float32)
    weights = (scores * causal).astype(jnp.bfloat16)
    intra = jnp.einsum("nhts,nshe->nthe", weights, value, preferred_element_type=jnp.float32)
    raw = inter + intra
    normal = (
        raw
        * lax.rsqrt(jnp.mean(raw * raw, axis=3, keepdims=True) + 1e-06)
        * out_gain.reshape(heads, size)
    )
    attended = normal.astype(jnp.bfloat16).reshape(rows, width)
    return (attended, carried + total)


def solution(mesh):
    return jax.shard_map(
        shards,
        mesh=mesh,
        in_specs=(
            P("seq", "tensor"),
            P(),
            P("seq", "tensor"),
            P("seq", "tensor"),
            P("seq", "tensor"),
            P("tensor"),
            P("tensor", None, None),
        ),
        out_specs=(P("seq", "tensor"), P("tensor", None, None)),
        check_vma=False,
    )
```

profile of v0, /device:TPU:1, one launch (start us, length us, event | category | flops | bytes accessed | tf_op | source)
XLA Modules:
  0.0 293.1 jit_solution(6839959478735101237)
XLA Ops:
  7.2 0.7 all-gather.7.cloned.1.call-update
  7.9 0.0 all-gather.9.cloned.1.call-start
  8.0 0.7 all-gather.9.cloned.1.call-update
  8.7 0.0 all-gather.11.cloned.1.call-start
  8.7 0.7 all-gather.11.cloned.1.call-update
  9.4 0.5 all-gather.13.cloned.1.call-update
  10.0 0.0 all-gather.15.cloned.1.call-start
  10.0 58.4 %all-gather.7.cloned.1.call-done = bf16[512,4096]{1,0:T(8,128)(2,1)} async-done(((bf16[512,512]{1,0:T(8,128)(2,1)}), bf16[512,4096]{1,0:T(8,128)(2,1)}) %all-gather.7.cloned.1.call-update) | async-done | bytes 4194320 | tf_op jit(solution)/shard_map/all_gather | solution.py:14
  68.5 3.1 %fusion = f32[512]{0:T(512)S(1)} fusion(bf16[512,4096]{1,0:T(8,128)(2,1)} %all-gather.7.cloned.1.call-done), kind=kLoop, calls=%fused_computation.4 | loop fusion | flops 6290944 | bytes 4196352 | tf_op jit(solution)/shard_map/reduce_sum | solution.py:16
  71.5 49.6 %all-gather.9.cloned.1.call-done = bf16[4096,512]{1,0:T(8,128)(2,1)} async-done(((bf16[128,512]{1,0:T(8,128)(2,1)}), bf16[4096,512]{1,0:T(8,128)(2,1)}) %all-gather.9.cloned.1.call-update) | async-done | bytes 4194320 | tf_op jit(solution)/shard_map/all_gather | solution.py:27
  121.2 5.9 %convolution_convert_fusion.2 = bf16[512,512]{0,1:T(8,128)(2,1)S(1)} fusion(bf16[4096,512]{1,0:T(8,128)(2,1)} %all-gather.9.cloned.1.call-done, bf16[512,4096]{1,0:T(8,128)(2,1)} %all-gather.7.cloned.1.call-done, f32[4096]{0:T(1024)S(1)} %copy-done.4, f32[512]{0:T(512)S(1)} %add_rsqrt_fusion.1), kind=kOutput, calls=%fused_computation.14 | convolution fusion | flops 2156134400 | bytes 8931328 | tf_op jit(solution)/shard_map/dot_general | solution.py:10
  127.1 47.2 %all-gather.11.cloned.1.call-done = bf16[4096,512]{1,0:T(8,128)(2,1)} async-done(((bf16[128,512]{1,0:T(8,128)(2,1)}), bf16[4096,512]{1,0:T(8,128)(2,1)}) %all-gather.11.cloned.1.call-update) | async-done | bytes 4194320 | tf_op jit(solution)/shard_map/all_gather | solution.py:28
  174.3 5.9 %convolution_convert_fusion.1 = bf16[512,512]{0,1:T(8,128)(2,1)S(1)} fusion(bf16[4096,512]{1,0:T(8,128)(2,1)} %all-gather.11.cloned.1.call-done, bf16[512,4096]{1,0:T(8,128)(2,1)} %all-gather.7.cloned.1.call-done, f32[4096]{0:T(1024)S(1)} %copy-done.4, f32[512]{0:T(512)S(1)} %add_rsqrt_fusion.1), kind=kOutput, calls=%fused_computation.13 | convolution fusion | flops 2156134400 | bytes 8931328 | tf_op jit(solution)/shard_map/dot_general | solution.py:10
  180.2 1.0 fusion.13
  181.3 0.1 fusion.6
  181.4 45.8 %all-gather.13.cloned.1.call-done = bf16[4096,512]{1,0:T(8,128)(2,1)} async-done(((bf16[128,512]{1,0:T(8,128)(2,1)}), bf16[4096,512]{1,0:T(8,128)(2,1)}) %all-gather.13.cloned.1.call-update) | async-done | bytes 4194320 | tf_op jit(solution)/shard_map/all_gather | solution.py:26
  227.2 6.7 %convolution_convert_fusion = bf16[512,512]{0,1:T(8,128)(2,1)} fusion(bf16[4096,512]{1,0:T(8,128)(2,1)} %all-gather.13.cloned.1.call-done, bf16[512,4096]{1,0:T(8,128)(2,1)} %all-gather.7.cloned.1.call-done, f32[4096]{0:T(1024)S(1)} %copy-done.4, f32[512]{0:T(512)S(1)} %add_rsqrt_fusion.1), kind=kOutput, calls=%fused_computation.12 | convolution fusion | flops 2156134400 | bytes 8931328 | tf_op jit(solution)/shard_map/dot_general | solution.py:10
  234.0 2.5 fusion.4
  236.5 43.7 %all-gather.15.cloned.1.call-done = bf16[128,128,128]{2,1,0:T(8,128)(2,1)} async-done(((bf16[4,128,128]{2,1,0:T(8,128)(2,1)}), bf16[128,128,128]{2,1,0:T(8,128)(2,1)}) %all-gather.15.cloned.1.call-update) | async-done | bytes 4194320 | tf_op jit(solution)/shard_map/all_gather | solution.py:39
  280.2 3.6 %convert_reduce_fusion = (f32[4,128,128]{2,1,0:T(8,128)S(1)}, f32[4,128,128]{2,1,0:T(8,128)S(1)}) fusion(bf16[32,4,128,128]{3,2,1,0:T(8,128)(2,1)} %bitcast.20, f32[32]{0:T(128)S(1)} %compare_convert_fusion), kind=kLoop, calls=%fused_computation | loop fusion | flops 8257536 | bytes 4718720 | tf_op jit(solution)/shard_map/reduce_sum | solution.py:45
  283.9 0.7 multiply_reduce_fusion
  284.6 0.2 multiply_convert_fusion.1
  284.8 1.0 copy.16
  285.8 0.7 add.52
  (16 shorter events, 0.1 us)
Async XLA Ops:
  7.2 114.0 %copy-start.4 = (f32[4096]{0:T(1024)S(1)}, f32[4096]{0:T(1024)}, u32[]{:S(2)}) copy-start(f32[4096]{0:T(1024)} %param.8) | copy-start | bytes 49156
  7.2 61.3 %all-gather.7.cloned.1.call-start = ((), (), s32[]{:S(2)}) async-start(), calls=%async_computation | async-start | bytes 4718592 | tf_op jit(solution)/shard_map/all_gather | solution.py:14
  7.9 113.2 %all-gather.9.cloned.1.call-start = ((), (), s32[]{:S(2)}) async-start(), calls=%async_computation.1 | async-start | bytes 4325376 | tf_op jit(solution)/shard_map/all_gather | solution.py:27
  8.7 165.6 %all-gather.11.cloned.1.call-start = ((), (), s32[]{:S(2)}) async-start(), calls=%async_computation.2 | async-start | bytes 4325376 | tf_op jit(solution)/shard_map/all_gather | solution.py:28
  9.4 217.8 %all-gather.13.cloned.1.call-start = ((), (), s32[]{:S(2)}) async-start(), calls=%async_computation.3 | async-start | bytes 4325376 | tf_op jit(solution)/shard_map/all_gather | solution.py:26
  10.0 270.2 %all-gather.15.cloned.1.call-start = ((), (), s32[]{:S(2)}) async-start(), calls=%async_computation.4 | async-start | bytes 4325376 | tf_op jit(solution)/shard_map/all_gather | solution.py:39
  234.0 49.9 %copy-start.1 = (f32[4,128,128]{2,1,0:T(8,128)S(1)}, f32[4,128,128]{2,1,0:T(8,128)}, u32[]{:S(2)}) copy-start(f32[4,128,128]{2,1,0:T(8,128)} %param.13) | copy-start | bytes 786436
  236.5 47.4 %copy-start = (bf16[512,512]{0,1:T(8,128)(2,1)S(1)}, bf16[512,512]{0,1:T(8,128)(2,1)}, u32[]{:S(2)}) copy-start(bf16[512,512]{0,1:T(8,128)(2,1)} %convolution_convert_fusion) | copy-start | bytes 1572868
  236.5 47.4 %copy-start.2 = (f32[4,128,128]{2,1,0:T(8,128)S(1)}, f32[4,128,128]{2,1,0:T(8,128)}, u32[]{:S(2)}) copy-start(f32[4,128,128]{2,1,0:T(8,128)} %get-tuple-element.9) | copy-start | bytes 786436
  236.5 48.1 %copy-start.3 = (f32[512]{0:T(512)S(1)}, f32[512]{0:T(512)}, u32[]{:S(2)}) copy-start(f32[512]{0:T(512)} %param.12) | copy-start | bytes 6148
Sparse Core Ops, SparseCore 0:
  9.8 58.6 all-gather.6
  71.0 50.0 all-gather.8
  123.7 50.5 all-gather.10
  176.7 50.5 all-gather.12
  229.6 50.5 all-gather.14
where the time goes:
time: 293 us
  waiting for transfers between devices  247 us (84%)
  matrix products  22.9 us (8%)
  between operations  13.9 us (5%)
  other arithmetic  7.74 us (3%)
    all_gather x1, waiting for transfers between devices, shards(): whole = lax.all_gather(tokens, 'tensor', axis=1, tiled=True)  58.4 us
    all_gather x1, waiting for transfers between devices, shards(): lax.all_gather(w_key, 'seq', axis=0, tiled=True)  49.6 us
    all_gather x1, waiting for transfers between devices, shards(): lax.all_gather(w_value, 'seq', axis=0, tiled=True)  47.2 us
    all_gather x1, waiting for transfers between devices, shards(): lax.all_gather(w_query, 'seq', axis=0, tiled=True)  45.8 us
    all_gather x1, waiting for transfers between devices, shards(): lax.all_gather(local_total[None].astype(jnp.bfloat16), 'seq', axis=0, til...  43.7 us
    dot_general x3, matrix products, add_rows(): jnp.dot(normed, piece, preferred_element_type=jnp.float32)  18.6 us
  transfers between devices with their start and end apart: 5, of which 5 were waited for; matrix products, arithmetic and copies ran while one was open for 9% of the time, Pallas kernels for 0%

commit v1 on v0

--- a/solution.py
+++ b/solution.py
@@ -11,7 +11,23 @@
 
 
 def shards(tokens, norm_gain, w_query, w_key, w_value, out_gain, carried):
-    whole = lax.all_gather(tokens, "tensor", axis=1, tiled=True)
+    ways, here, turn = (lax.axis_size("tensor"), lax.axis_index("tensor"), tokens.shape[1])
+    shape = [n * ways if d == 1 else n for d, n in enumerate(tokens.shape)]
+    full = lax.dynamic_update_slice_in_dim(
+        jnp.zeros(shape, tokens.dtype), tokens, here * turn, axis=1
+    )
+    going_up = going_down = tokens
+    for far in range(1, ways // 2 + 1):
+        going_up = lax.ppermute(going_up, "tensor", [(d, (d + 1) % ways) for d in range(ways)])
+        full = lax.dynamic_update_slice_in_dim(full, going_up, (here - far) % ways * turn, axis=1)
+        if 2 * far < ways:
+            going_down = lax.ppermute(
+                going_down, "tensor", [(d, (d - 1) % ways) for d in range(ways)]
+            )
+            full = lax.dynamic_update_slice_in_dim(
+                full, going_down, (here + far) % ways * turn, axis=1
+            )
+    whole = full
     xf = whole.astype(jnp.float32)
     normed = (xf * lax.rsqrt(jnp.mean(xf * xf, axis=1, keepdims=True) + 1e-05) * norm_gain).astype(
         jnp.bfloat16

time: 293 us -> 238 us (0.81)
  waiting for transfers between devices: 247 us -> 179 us
  starting transfers between devices: 0.19 us -> 12.2 us
  local copies, waits for them, and re-layouts: 1.03 us -> 4.02 us
    all_gather x1 -> x0, waiting for transfers between devices: 58.4 us -> none  [shards(): whole = lax.all_gather(tokens, 'tensor', axis=1, tiled=True)]
    all_gather x1, waiting for transfers between devices: 49.6 us -> 0.02 us  [shards(): lax.all_gather(w_key, 'seq', axis=0, tiled=True)]
    ppermute x0 -> x7, waiting for transfers between devices: none -> 42.9 us  [the longest x4 42.9 us: shards(): lax.ppermute(going_up, 'tensor', [(d, (d + 1) % ways) for d in range(ways)])]
    ppermute x0 -> x7, starting transfers between devices: none -> 12 us  [the longest x3 9.45 us: shards(): lax.ppermute(going_down, 'tensor', [(d, (d - 1) % ways) for d in range(wa...]
  transfers between devices with their start and end apart: 5 -> 11, of which waited for: 5 -> 7; matrix products, arithmetic and copies ran while one was open for 9% -> 10% of each run, Pallas kernels for 0% -> 0%
where the time goes in v1:
time: 238 us
  waiting for transfers between devices  179 us (75%)
  matrix products  22.8 us (10%)
  between operations  14 us (6%)
  starting transfers between devices  12.2 us (5%)
  other arithmetic  5.54 us (2%)
  local copies, waits for them, and re-layouts  4.02 us (2%)
    all_gather x1, waiting for transfers between devices, shards(): lax.all_gather(w_query, 'seq', axis=0, tiled=True)  46 us
    all_gather x1, waiting for transfers between devices, shards(): lax.all_gather(w_value, 'seq', axis=0, tiled=True)  44.7 us
    all_gather x1, waiting for transfers between devices, shards(): lax.all_gather(local_total[None].astype(jnp.bfloat16), 'seq', axis=0, til...  43.7 us
    ppermute x4, waiting for transfers between devices, shards(): lax.ppermute(going_up, 'tensor', [(d, (d + 1) % ways) for d in range(ways)])  42.9 us
    dot_general x3, matrix products, add_rows(): jnp.dot(normed, piece, preferred_element_type=jnp.float32)  18.6 us
    ppermute x3, starting transfers between devices, shards(): lax.ppermute(going_down, 'tensor', [(d, (d - 1) % ways) for d in range(wa...  9.45 us
  transfers between devices with their start and end apart: 11, of which 7 were waited for; matrix products, arithmetic and copies ran while one was open for 10% of the time, Pallas kernels for 0%

profile of v1, /device:TPU:1, one launch (start us, length us, event | category | flops | bytes accessed | tf_op | source)
XLA Modules:
  0.0 237.9 jit_solution(14697168734150610838)
XLA Ops:
  7.2 0.7 all-gather.6.cloned.1.call-update
  8.0 0.7 all-gather.8.cloned.1.call-update
  9.4 2.5 %collective-permute-start = (bf16[512,512]{1,0:T(8,128)(2,1)}, bf16[512,512]{1,0:T(8,128)(2,1)S(1)}, u32[]{:S(2)}, u32[]{:S(2)}) collective-permute-start(bf16[512,512]{1,0:T(8,128)(2,1)} %param.7), channel_id=1, source_target_pairs={{0,1},{1,2},{2,3},{3,4},{4,5},{5,6},{6,7},{7,0},{8,9},{9,10},{10,1... | collective-permute-start | bytes 1572872 | tf_op jit(solution)/shard_map/ppermute | solution.py:21
  12.0 4.0 %collective-permute-start.1 = (bf16[512,512]{1,0:T(8,128)(2,1)}, bf16[512,512]{1,0:T(8,128)(2,1)S(1)}, u32[]{:S(2)}, u32[]{:S(2)}) collective-permute-start(bf16[512,512]{1,0:T(8,128)(2,1)} %param.7), channel_id=1, source_target_pairs={{0,7},{1,0},{2,1},{3,2},{4,3},{5,4},{6,5},{7,6},{8,15},{9,8},{10,9... | collective-permute-start | bytes 1572872 | tf_op jit(solution)/shard_map/ppermute | solution.py:24
  16.0 11.8 %collective-permute-done = bf16[512,512]{1,0:T(8,128)(2,1)S(1)} collective-permute-done((bf16[512,512]{1,0:T(8,128)(2,1)}, bf16[512,512]{1,0:T(8,128)(2,1)S(1)}, u32[]{:S(2)}, u32[]{:S(2)}) %collective-permute-start) | collective-permute-done | bytes 524320 | tf_op jit(solution)/shard_map/ppermute | solution.py:21
  27.8 2.7 %collective-permute-start.3 = (bf16[512,512]{1,0:T(8,128)(2,1)S(1)}, bf16[512,512]{1,0:T(8,128)(2,1)S(1)}, u32[]{:S(2)}, u32[]{:S(2)}) collective-permute-start(bf16[512,512]{1,0:T(8,128)(2,1)S(1)} %collective-permute-done.1), channel_id=1, source_target_pairs={{0,7},{1,0},{2,1},{3,2},{4,3},{5,4},{6,5},{7,6},{8,15},{9,8},{10,9... | collective-permute-start | bytes 1572872 | tf_op jit(solution)/shard_map/ppermute | solution.py:24
  30.5 10.7 %collective-permute-done.2 = bf16[512,512]{1,0:T(8,128)(2,1)S(1)} collective-permute-done((bf16[512,512]{1,0:T(8,128)(2,1)S(1)}, bf16[512,512]{1,0:T(8,128)(2,1)S(1)}, u32[]{:S(2)}, u32[]{:S(2)}) %collective-permute-start.2) | collective-permute-done | bytes 524320 | tf_op jit(solution)/shard_map/ppermute | solution.py:21
  41.8 2.7 %collective-permute-start.5 = (bf16[512,512]{1,0:T(8,128)(2,1)S(1)}, bf16[512,512]{1,0:T(8,128)(2,1)S(1)}, u32[]{:S(2)}, u32[]{:S(2)}) collective-permute-start(bf16[512,512]{1,0:T(8,128)(2,1)S(1)} %collective-permute-done.3), channel_id=1, source_target_pairs={{0,7},{1,0},{2,1},{3,2},{4,3},{5,4},{6,5},{7,6},{8,15},{9,8},{10,9... | collective-permute-start | bytes 1572872 | tf_op jit(solution)/shard_map/ppermute | solution.py:24
  44.6 9.2 %collective-permute-done.4 = bf16[512,512]{1,0:T(8,128)(2,1)S(1)} collective-permute-done((bf16[512,512]{1,0:T(8,128)(2,1)S(1)}, bf16[512,512]{1,0:T(8,128)(2,1)S(1)}, u32[]{:S(2)}, u32[]{:S(2)}) %collective-permute-start.4) | collective-permute-done | bytes 524320 | tf_op jit(solution)/shard_map/ppermute | solution.py:21
  54.2 11.3 %collective-permute-done.6 = bf16[512,512]{1,0:T(8,128)(2,1)S(1)} collective-permute-done((bf16[512,512]{1,0:T(8,128)(2,1)S(1)}, bf16[512,512]{1,0:T(8,128)(2,1)S(1)}, u32[]{:S(2)}, u32[]{:S(2)}) %collective-permute-start.6) | collective-permute-done | bytes 524320 | tf_op jit(solution)/shard_map/ppermute | solution.py:21
  65.5 2.0 copy-done
  67.5 0.9 fusion
  68.4 5.9 %convolution_convert_fusion.2 = bf16[512,512]{0,1:T(8,128)(2,1)S(1)} fusion(bf16[4096,512]{1,0:T(8,128)(2,1)} %all-gather.6.cloned.1.call-done, bf16[512,4096]{1,0:T(8,128)(2,1)} %copy-done, f32[4096]{0:T(1024)S(1)} %copy-done.6, f32[512]{0:T(512)S(1)} %add_rsqrt_fusion.1), kind=kOutput, calls=%fused_computation.14 | convolution fusion | flops 2156134400 | bytes 8931328 | tf_op jit(solution)/shard_map/dot_general | solution.py:10
  74.3 44.7 %all-gather.8.cloned.1.call-done = bf16[4096,512]{1,0:T(8,128)(2,1)} async-done(((bf16[128,512]{1,0:T(8,128)(2,1)}), bf16[4096,512]{1,0:T(8,128)(2,1)}) %all-gather.8.cloned.1.call-update) | async-done | bytes 4194320 | tf_op jit(solution)/shard_map/all_gather | solution.py:44
  119.0 5.9 %convolution_convert_fusion.1 = bf16[512,512]{0,1:T(8,128)(2,1)S(1)} fusion(bf16[4096,512]{1,0:T(8,128)(2,1)} %all-gather.8.cloned.1.call-done, bf16[512,4096]{1,0:T(8,128)(2,1)} %copy-done, f32[4096]{0:T(1024)S(1)} %copy-done.6, f32[512]{0:T(512)S(1)} %add_rsqrt_fusion.1), kind=kOutput, calls=%fused_computation.13 | convolution fusion | flops 2156134400 | bytes 8931328 | tf_op jit(solution)/shard_map/dot_general | solution.py:10
  124.9 1.0 fusion.13
  126.1 46.0 %all-gather.10.cloned.1.call-done = bf16[4096,512]{1,0:T(8,128)(2,1)} async-done(((bf16[128,512]{1,0:T(8,128)(2,1)}), bf16[4096,512]{1,0:T(8,128)(2,1)}) %all-gather.10.cloned.1.call-update) | async-done | bytes 4194320 | tf_op jit(solution)/shard_map/all_gather | solution.py:42
  172.1 6.7 %convolution_convert_fusion = bf16[512,512]{0,1:T(8,128)(2,1)} fusion(bf16[4096,512]{1,0:T(8,128)(2,1)} %all-gather.10.cloned.1.call-done, bf16[512,4096]{1,0:T(8,128)(2,1)} %copy-done, f32[4096]{0:T(1024)S(1)} %copy-done.6, f32[512]{0:T(512)S(1)} %add_rsqrt_fusion.1), kind=kOutput, calls=%fused_computation.12 | convolution fusion | flops 2156134400 | bytes 8931328 | tf_op jit(solution)/shard_map/dot_general | solution.py:10
  178.8 2.5 %fusion.4 = f32[4,128,512]{2,1,0:T(8,128)S(1)} fusion(bf16[512,4,128]{0,2,1:T(8,128)(2,1)S(1)} %bitcast.24, bf16[512,4,128]{0,2,1:T(8,128)(2,1)} %bitcast.25, bf16[512,4,128]{0,2,1:T(8,128)(2,1)S(1)} %bitcast.22, f32[512,512]{1,0:T(8,128)S(1)} %fusion.6), kind=kOutput, calls=%fused_computation.9 | convolution fusion | flops 538968064 | bytes 3670016 | tf_op jit(solution)/shard_map/nhts,nshe->nthe/dot_general | solution.py:71
  181.4 43.7 %all-gather.12.cloned.1.call-done = bf16[128,128,128]{2,1,0:T(8,128)(2,1)} async-done(((bf16[4,128,128]{2,1,0:T(8,128)(2,1)}), bf16[128,128,128]{2,1,0:T(8,128)(2,1)}) %all-gather.12.cloned.1.call-update) | async-done | bytes 4194320 | tf_op jit(solution)/shard_map/all_gather | solution.py:55
  225.1 3.6 %convert_reduce_fusion = (f32[4,128,128]{2,1,0:T(8,128)S(1)}, f32[4,128,128]{2,1,0:T(8,128)S(1)}) fusion(bf16[32,4,128,128]{3,2,1,0:T(8,128)(2,1)} %bitcast.20, f32[32]{0:T(128)S(1)} %compare_convert_fusion), kind=kLoop, calls=%fused_computation | loop fusion | flops 8257536 | bytes 4718720 | tf_op jit(solution)/shard_map/reduce_sum | solution.py:61
  228.8 0.7 multiply_reduce_fusion
  229.6 1.0 copy.16
  230.7 0.7 add.129
  (40 shorter events, 2.2 us)
Async XLA Ops:
  7.2 34.5 %copy-start.4 = (bf16[512,512]{1,0:T(8,128)(2,1)S(1)}, bf16[512,512]{1,0:T(8,128)(2,1)}, u32[]{:S(2)}) copy-start(bf16[512,512]{1,0:T(8,128)(2,1)} %param.7) | copy-start | bytes 1572868
  7.2 61.2 %all-gather.6.cloned.1.call-start = ((), (), s32[]{:S(2)}) async-start(), calls=%async_computation | async-start | bytes 4325376 | tf_op jit(solution)/shard_map/all_gather | solution.py:43
  7.9 111.1 %all-gather.8.cloned.1.call-start = ((), (), s32[]{:S(2)}) async-start(), calls=%async_computation.1 | async-start | bytes 4325376 | tf_op jit(solution)/shard_map/all_gather | solution.py:44
  8.7 163.5 %all-gather.10.cloned.1.call-start = ((), (), s32[]{:S(2)}) async-start(), calls=%async_computation.2 | async-start | bytes 4325376 | tf_op jit(solution)/shard_map/all_gather | solution.py:42
  9.4 215.7 %all-gather.12.cloned.1.call-start = ((), (), s32[]{:S(2)}) async-start(), calls=%async_computation.3 | async-start | bytes 4325376 | tf_op jit(solution)/shard_map/all_gather | solution.py:55
  9.4 18.3 %collective-permute-start = (bf16[512,512]{1,0:T(8,128)(2,1)}, bf16[512,512]{1,0:T(8,128)(2,1)S(1)}, u32[]{:S(2)}, u32[]{:S(2)}) collective-permute-start(bf16[512,512]{1,0:T(8,128)(2,1)} %param.7), channel_id=1, source_target_pairs={{0,1},{1,2},{2,3},{3,4},{4,5},{5,6},{6,7},{7,0},{8,9},{9,10},{10,1... | collective-permute-start | bytes 1572872 | tf_op jit(solution)/shard_map/ppermute | solution.py:21
  12.0 15.8 %collective-permute-start.1 = (bf16[512,512]{1,0:T(8,128)(2,1)}, bf16[512,512]{1,0:T(8,128)(2,1)S(1)}, u32[]{:S(2)}, u32[]{:S(2)}) collective-permute-start(bf16[512,512]{1,0:T(8,128)(2,1)} %param.7), channel_id=1, source_target_pairs={{0,7},{1,0},{2,1},{3,2},{4,3},{5,4},{6,5},{7,6},{8,15},{9,8},{10,9... | collective-permute-start | bytes 1572872 | tf_op jit(solution)/shard_map/ppermute | solution.py:24
  27.8 13.4 %collective-permute-start.2 = (bf16[512,512]{1,0:T(8,128)(2,1)S(1)}, bf16[512,512]{1,0:T(8,128)(2,1)S(1)}, u32[]{:S(2)}, u32[]{:S(2)}) collective-permute-start(bf16[512,512]{1,0:T(8,128)(2,1)S(1)} %collective-permute-done), channel_id=1, source_target_pairs={{0,1},{1,2},{2,3},{3,4},{4,5},{5,6},{6,7},{7,0},{8,9},{9,10},{10,1... | collective-permute-start | bytes 1572872 | tf_op jit(solution)/shard_map/ppermute | solution.py:21
  27.8 14.0 %collective-permute-start.3 = (bf16[512,512]{1,0:T(8,128)(2,1)S(1)}, bf16[512,512]{1,0:T(8,128)(2,1)S(1)}, u32[]{:S(2)}, u32[]{:S(2)}) collective-permute-start(bf16[512,512]{1,0:T(8,128)(2,1)S(1)} %collective-permute-done.1), channel_id=1, source_target_pairs={{0,7},{1,0},{2,1},{3,2},{4,3},{5,4},{6,5},{7,6},{8,15},{9,8},{10,9... | collective-permute-start | bytes 1572872 | tf_op jit(solution)/shard_map/ppermute | solution.py:24
  41.2 12.6 %collective-permute-start.4 = (bf16[512,512]{1,0:T(8,128)(2,1)S(1)}, bf16[512,512]{1,0:T(8,128)(2,1)S(1)}, u32[]{:S(2)}, u32[]{:S(2)}) collective-permute-start(bf16[512,512]{1,0:T(8,128)(2,1)S(1)} %collective-permute-done.2), channel_id=1, source_target_pairs={{0,1},{1,2},{2,3},{3,4},{4,5},{5,6},{6,7},{7,0},{8,9},{9,10},{10,1... | collective-permute-start | bytes 1572872 | tf_op jit(solution)/shard_map/ppermute | solution.py:21
  41.8 12.3 %collective-permute-start.5 = (bf16[512,512]{1,0:T(8,128)(2,1)S(1)}, bf16[512,512]{1,0:T(8,128)(2,1)S(1)}, u32[]{:S(2)}, u32[]{:S(2)}) collective-permute-start(bf16[512,512]{1,0:T(8,128)(2,1)S(1)} %collective-permute-done.3), channel_id=1, source_target_pairs={{0,7},{1,0},{2,1},{3,2},{4,3},{5,4},{6,5},{7,6},{8,15},{9,8},{10,9... | collective-permute-start | bytes 1572872 | tf_op jit(solution)/shard_map/ppermute | solution.py:24
  53.8 11.7 %collective-permute-start.6 = (bf16[512,512]{1,0:T(8,128)(2,1)S(1)}, bf16[512,512]{1,0:T(8,128)(2,1)S(1)}, u32[]{:S(2)}, u32[]{:S(2)}) collective-permute-start(bf16[512,512]{1,0:T(8,128)(2,1)S(1)} %collective-permute-done.4), channel_id=1, source_target_pairs={{0,1},{1,2},{2,3},{3,4},{4,5},{5,6},{6,7},{7,0},{8,9},{9,10},{10,1... | collective-permute-start | bytes 1572872 | tf_op jit(solution)/shard_map/ppermute | solution.py:21
  53.9 14.5 %copy-start.6 = (f32[4096]{0:T(1024)S(1)}, f32[4096]{0:T(1024)}, u32[]{:S(2)}) copy-start(f32[4096]{0:T(1024)} %param.8) | copy-start | bytes 49156
  65.5 2.0 copy-start
  178.8 49.9 %copy-start.2 = (f32[4,128,128]{2,1,0:T(8,128)S(1)}, f32[4,128,128]{2,1,0:T(8,128)}, u32[]{:S(2)}) copy-start(f32[4,128,128]{2,1,0:T(8,128)} %param.13) | copy-start | bytes 786436
  181.3 47.4 %copy-start.1 = (bf16[512,512]{0,1:T(8,128)(2,1)S(1)}, bf16[512,512]{0,1:T(8,128)(2,1)}, u32[]{:S(2)}) copy-start(bf16[512,512]{0,1:T(8,128)(2,1)} %convolution_convert_fusion) | copy-start | bytes 1572868
  181.3 47.4 %copy-start.3 = (f32[4,128,128]{2,1,0:T(8,128)S(1)}, f32[4,128,128]{2,1,0:T(8,128)}, u32[]{:S(2)}) copy-start(f32[4,128,128]{2,1,0:T(8,128)} %get-tuple-element.9) | copy-start | bytes 786436
  181.3 48.1 %copy-start.5 = (f32[512]{0:T(512)S(1)}, f32[512]{0:T(512)}, u32[]{:S(2)}) copy-start(f32[512]{0:T(512)} %param.12) | copy-start | bytes 6148
Sparse Core Ops, SparseCore 0:
  10.6 55.2 all-gather.5
  68.5 50.5 all-gather.7
  121.6 50.5 all-gather.9
  174.5 50.5 all-gather.11
